TPU v7x, 32 devices: a whole 2x2x4 slice. The times are simulated.
32 devices in a mesh: row: 8 (over z, y), col: 4 (over x, core).
Axes of the slice: x: 2, y: 2, z: 4, core: 2. Of those that a mesh axis runs over, the one named last changes fastest.
Arguments:
- jacobian: float32 [16384, 16384], P('row', 'col'), may hold values from -6 to 6
- diff_inputs: float32 [32768, 128], P('row'), may hold values from -0.00390625 to 0.00390625
- diff_outputs: float32 [32768, 128], P('row'), may hold values from -6 to 6
- face_dof: int32 [32768], P('row'), may hold values from 0 to 16383, as said below
- counts: int32 [8], P('row'), may hold values from 128 to 4096, as said below
- residual: float32 [16384], P('col'), may hold values from -0.046875 to 0.046875
- trial: float32 [16384], P('row'), may hold values from -6 to 6
Outputs:
- updated: float32 [16384, 16384], P('row', 'col')
- corrected: float32 [16384], P('row')
Inputs may be any that keep to these rules, and one draw needn't show every extreme that they name: Each owner's count is a multiple of 128; the counts sum to 16384; some owner holds exactly 4096. `face_dof`: live slots name every degree of freedom exactly once over all owners, in runs of 128 consecutive degrees of freedom starting at multiples of 128; slots at or past an owner's count hold arbitrary values that belong to no column.
All inputs are finite; a program needn't handle non-finite values. Where the computation divides by a largest or mean magnitude, that divisor is 1e-20 or more.
Results may differ from a plain program's by a relative error of at most 0.0001.
Values sent between devices are 32-bit elements; how exact they have to be, the bound alone decides.
A program may use at most 192 MiB of HBM per device.

v0:
```python
import functools

import jax
import jax.numpy as jnp
from jax import lax
from jax.experimental import pallas as pl
from jax.experimental.pallas import tpu as pltpu
from jax.sharding import PartitionSpec as P

K = 128
NS = 4
UNIT = 128
TILE = 256

HIGH = lax.Precision.HIGHEST
REG = 0.1
F32 = jnp.float32
BF16 = jnp.bfloat16
MESH = pl.DeviceIdType.MESH
VMEM_SPEC = pl.BlockSpec(memory_space=pltpu.VMEM)
SMEM_SPEC = pl.BlockSpec(memory_space=pltpu.SMEM)


def split(x):
    hi = x.astype(BF16)
    return hi, (x - hi.astype(F32)).astype(BF16)


def ring_place(index, n):
    return index // 2 + (index % 2) * (n - 1 - 2 * (index // 2))


def ring_index(place, n):
    side = place // (n // 2)
    level = place + side * (n - 1 - 2 * place)
    return 2 * level + side


def ring_kernel(
    n, parts, src_ref, mask_ref, x_ref, r_ref, vb_ref, vt_ref, gb_ref,
    whole, landed, sent, gram, beta, send_sem, recv_sem,
):
    place = ring_place(lax.axis_index("row"), n)
    right = ring_index((place + 1) % n, n)
    left = ring_index((place + n - 1) % n, n)
    barrier = pltpu.get_barrier_semaphore()
    for peer in (left, right):
        pl.semaphore_signal(barrier, inc=1, device_id={"row": peer}, device_id_type=MESH)
    pl.semaphore_wait(barrier, 2)

    def granule(way, back, part):
        sign = 1 if way == 0 else -1
        chunk = (place + 2 * n - sign * back) % n
        return (way * n + chunk) * parts + part

    def own(at):
        return x_ref[src_ref[at]] * mask_ref[at]

    def copy(step, way, part, source, target):
        return pltpu.make_async_remote_copy(
            src_ref=source,
            dst_ref=target,
            send_sem=send_sem.at[way, step, part],
            recv_sem=recv_sem.at[way, step, part],
            device_id={"row": right if way == 0 else left},
            device_id_type=MESH,
        )

    per_unit = UNIT // whole.shape[1]

    def absorb(unit):
        rows = jnp.concatenate([whole[unit * per_unit + sub] for sub in range(per_unit)], axis=0)
        at = pl.ds(pl.multiple_of(unit * UNIT, UNIT), UNIT)
        hi, lo = split(rows)
        both = jnp.concatenate([hi, lo], axis=1)
        vb_ref[at, :] = both
        t_hi, t_lo = split(jnp.transpose(rows))
        vt_ref[:K, at] = t_hi
        vt_ref[K:, at] = t_lo
        gram[...] += lax.dot_general(
            both, both, (((0,), (0,)), ((), ())), preferred_element_type=F32
        )
        r_hi, r_lo = split(jnp.broadcast_to(r_ref[:, at], (8, UNIT)))
        beta[...] += jnp.dot(
            jnp.concatenate([r_hi, r_lo], axis=0), both, preferred_element_type=F32
        )

    gram[...] = jnp.zeros_like(gram)
    beta[...] = jnp.zeros_like(beta)
    copies = {}
    last = 2 * (n - 1)
    for step in range(last + 1):
        for part in range(parts):
            for way in range(2):
                if step > 0:
                    copies[step - 1, way, part].wait_recv()
                at = granule(way, step, part)
                if step < n - 1:
                    value = own(at)
                    if step > 0:
                        value = value + landed[way, step - 1, part]
                    sent[way, step, part] = value
                    source, target = sent.at[way, step, part], landed.at[way, step, part]
                else:
                    if step == n - 1:
                        whole[at] = own(at) + landed[way, step - 1, part]
                    source, target = whole.at[at], whole.at[at]
                if step < last:
                    copies[step, way, part] = copy(step, way, part, source, target)
                    copies[step, way, part].start()
                if step >= n - 1 and per_unit == 1:
                    absorb(at)
    if per_unit > 1:
        for unit in range(whole.shape[0] // per_unit):
            absorb(unit)
    gb_ref[:K, :] = gram[:K, :K] + (gram[:K, K:] + gram[K:, :K]) + gram[K:, K:]
    gb_ref[K:, :] = beta[:8, :K] + (beta[:8, K:] + beta[8:, :K])
    for key in copies:
        copies[key].wait_send()


def ring_sum(src, mask, x, residual, rows, n):
    chunk = rows // (2 * n)
    part = min(UNIT, chunk)
    parts = chunk // part
    return pl.pallas_call(
        functools.partial(ring_kernel, n, parts),
        out_shape=(
            jax.ShapeDtypeStruct((rows, 2 * K), BF16),
            jax.ShapeDtypeStruct((2 * K, rows), BF16),
            jax.ShapeDtypeStruct((K + 8, K), F32),
        ),
        in_specs=[SMEM_SPEC, SMEM_SPEC, VMEM_SPEC, VMEM_SPEC],
        out_specs=(VMEM_SPEC, VMEM_SPEC, VMEM_SPEC),
        scratch_shapes=[
            pltpu.VMEM((rows // part, part, K), F32),
            pltpu.VMEM((2, n - 1, parts, part, K), F32),
            pltpu.VMEM((2, n - 1, parts, part, K), F32),
            pltpu.VMEM((2 * K, 2 * K), F32),
            pltpu.VMEM((16, 2 * K), F32),
            pltpu.SemaphoreType.DMA((2, 2 * (n - 1), parts)),
            pltpu.SemaphoreType.DMA((2, 2 * (n - 1), parts)),
        ],
        compiler_params=pltpu.CompilerParams(collective_id=0, has_side_effects=True),
    )(src, mask, x.reshape(-1, part, K), residual)


def lookup(run_unit, wanted):
    hit = run_unit[None, :] == wanted[:, None]
    src = jnp.sum(jnp.where(hit, jnp.arange(run_unit.shape[0], dtype=jnp.int32)[None, :], 0), axis=1)
    return src.astype(jnp.int32), jnp.any(hit, axis=1).astype(F32)


def product_kernel(
    n, nc, parts, src_ref, mask_ref, x_ref, gb_ref, r_ref, vb_ref, j_ref,
    u_ref, beta_ref, jr_ref,
    w_land, w_sent, w_share, jv, jv_land, jr_all, gb_all, u_all,
    w_send, w_recv, jv_send, jv_recv, gb_send, gb_recv, jr_send, jr_recv, u_send, u_recv,
):
    tiles = jr_all.shape[1]
    tile = jr_all.shape[2]
    share = jv_land.shape[1]
    per_share = share // tile
    grain = w_share.shape[2]
    step_now = pl.program_id(0)
    me = lax.axis_index("col")
    place = ring_place(lax.axis_index("row"), n)
    right = ring_index((place + 1) % n, n)
    left = ring_index((place + n - 1) % n, n)
    peers = [(me + k) % nc for k in range(1, nc)]

    def to_col(source, target, send, recv, peer):
        return pltpu.make_async_remote_copy(
            src_ref=source, dst_ref=target, send_sem=send, recv_sem=recv,
            device_id={"col": peer}, device_id_type=MESH,
        )

    def gb_copy(k, slot):
        return to_col(gb_ref, gb_all.at[slot], gb_send.at[k], gb_recv.at[slot], peers[k])

    def jr_copy(k, slot):
        return to_col(jr_all.at[slot], jr_all.at[slot], jr_send.at[k], jr_recv.at[slot], peers[k])

    def jv_copy(at, sender, owner):
        rows = pl.ds(pl.multiple_of((at % per_share) * tile, tile), tile)
        return to_col(
            jv.at[at], jv_land.at[sender, rows], jv_send.at[at],
            jv_recv.at[sender, at % per_share], owner,
        )

    def w_copy(step, way, part):
        return pltpu.make_async_remote_copy(
            src_ref=w_sent.at[way, step, part], dst_ref=w_land.at[way, step, part],
            send_sem=w_send.at[way, step, part], recv_sem=w_recv.at[way, step, part],
            device_id={"row": right if way == 0 else left}, device_id_type=MESH,
        )

    def w_step(step):
        for part in range(parts):
            for way in range(2):
                sign = 1 if way == 0 else -1
                block = ring_index((place + 2 * n - sign * (step + 1)) % n, n)
                at = (block * 2 + way) * parts + part
                value = x_ref[src_ref[at]] * mask_ref[at]
                if step > 0:
                    w_copy(step - 1, way, part).wait_recv()
                    value = value + w_land[way, step - 1, part]
                if step < n - 1:
                    w_sent[way, step, part] = value
                    w_copy(step, way, part).start()
                else:
                    w_share[way, part] = value

    @pl.when(step_now == 0)
    def _():
        barrier = pltpu.get_barrier_semaphore()
        for peer in (left, right):
            pl.semaphore_signal(barrier, inc=1, device_id={"row": peer}, device_id_type=MESH)
        for peer in peers:
            pl.semaphore_signal(barrier, inc=1, device_id={"col": peer}, device_id_type=MESH)
        pl.semaphore_wait(barrier, 2 + len(peers))
        gb_all[me] = gb_ref[...]
        for k in range(nc - 1):
            gb_copy(k, me).start()

    each = -(-n // tiles)
    for at in range(tiles):
        @pl.when(step_now == at)
        def _():
            for step in range(at * each, min(n, (at + 1) * each)):
                w_step(step)

    hi, lo = split(j_ref[...])
    both = jnp.dot(jnp.concatenate([hi, lo], axis=0), vb_ref[...], preferred_element_type=F32)
    jv_tile = both[:tile, :K] + (both[:tile, K:] + both[tile:, :K]) + both[tile:, K:]
    total = jnp.zeros((tile, K), F32)
    for at in range(0, j_ref.shape[1], K):
        total = total + j_ref[:, at : at + K] * r_ref[:, at : at + K]
    jr_all[me, pl.ds(step_now, 1), :] = jnp.sum(jnp.transpose(total), axis=0, keepdims=True)
    jv[step_now] = jv_tile
    owner = step_now // per_share

    @pl.when(owner != me)
    def _():
        jv_copy(step_now, me, owner).start()

    @pl.when(owner == me)
    def _():
        rows = pl.ds(pl.multiple_of((step_now % per_share) * tile, tile), tile)
        jv_land[me, rows] = jv_tile

    @pl.when(step_now == tiles - 1)
    def _():
        for k in range(nc - 1):
            jr_copy(k, me).start()
        for k in range(nc - 1):
            gb_copy(k, peers[k]).wait_recv()
        sums = gb_all[0]
        for slot in range(1, nc):
            sums = sums + gb_all[slot]
        beta_ref[...] = sums[K:]
        gram = sums[:K]
        eye = (
            lax.broadcasted_iota(jnp.int32, (K, K), 0) == lax.broadcasted_iota(jnp.int32, (K, K), 1)
        ).astype(F32)
        trace = jnp.sum(jnp.sum(gram * eye, axis=0, keepdims=True), axis=1, keepdims=True)
        regular = gram + REG * (trace / K) * eye
        norm_one = jnp.max(
            jnp.sum(jnp.abs(regular), axis=0, keepdims=True), axis=1, keepdims=True
        )
        zmat = regular / (norm_one * norm_one)
        for sweep in range(NS):
            inner = jnp.dot(regular, zmat, precision=HIGH, preferred_element_type=F32)
            zmat = jnp.dot(zmat, 2.0 * eye - inner, precision=HIGH, preferred_element_type=F32)

        for k in range(nc - 1):
            for at in range(per_share):
                jv_copy(at, peers[k], me).wait_recv()
        for way in range(2):
            for part in range(parts):
                at = (way * parts + part) * grain
                jv_sum = jnp.zeros((grain, K), F32)
                for slot in range(nc):
                    jv_sum = jv_sum + jv_land[slot, at : at + grain]
                u_all[me, at : at + grain] = jnp.dot(
                    w_share[way, part] - jv_sum, zmat, precision=HIGH, preferred_element_type=F32
                )

        partner = me + 1 - 2 * (me % 2)

        def u_copy(slot, hop, peer):
            return to_col(
                u_all.at[slot], u_all.at[slot], u_send.at[hop], u_recv.at[slot], peer
            )

        half = nc // 2
        far = [(me + 2 * k) % nc for k in range(1, half)]
        for k, peer in enumerate(far):
            u_copy(me, k, peer).start()
        u_copy(me, half - 1, partner).start()
        for k in range(1, half):
            slot = (me + 2 * k) % nc
            u_copy(slot, half - 1 + k, partner).wait_recv()
            u_copy(slot, half - 1 + k, partner).start()

        for k in range(nc - 1):
            jr_copy(k, peers[k]).wait_recv()
        jr_sum = jr_all[0]
        for slot in range(1, nc):
            jr_sum = jr_sum + jr_all[slot]
        jr_ref[...] = jr_sum

        for k in range(half):
            slot = (partner + 2 * k) % nc
            u_copy(slot, 0, partner).wait_recv()
        u_ref[...] = u_all[...]
        for hop in range(nc - 1):
            u_copy(me, hop, partner).wait_send()
        for k in range(nc - 1):
            gb_copy(k, me).wait_send()
            jr_copy(k, me).wait_send()
            for at in range(per_share):
                jv_copy(peers[k] * per_share + at, me, peers[k]).wait_send()
        for step in range(n - 1):
            for part in range(parts):
                for way in range(2):
                    w_copy(step, way, part).wait_send()


def products(jacobian, vb, gb, residual, src, mask, x, grain, n, nc):
    rows, cols = jacobian.shape
    share = rows // nc
    tile = min(TILE, share)
    tiles = rows // tile
    parts = share // (2 * grain)
    dma = pltpu.SemaphoreType.DMA
    whole = lambda shape: pl.BlockSpec(shape, lambda i: (0,) * len(shape))
    out_shape = (
        jax.ShapeDtypeStruct((nc, share, K), F32),
        jax.ShapeDtypeStruct((8, K), F32),
        jax.ShapeDtypeStruct((tiles, tile), F32),
    )
    return pl.pallas_call(
        functools.partial(product_kernel, n, nc, parts),
        grid=(tiles,),
        out_shape=out_shape,
        in_specs=[
            SMEM_SPEC, SMEM_SPEC, VMEM_SPEC, VMEM_SPEC, VMEM_SPEC, VMEM_SPEC,
            pl.BlockSpec((tile, cols), lambda i: (i, 0)),
        ],
        out_specs=(VMEM_SPEC, VMEM_SPEC, VMEM_SPEC),
        scratch_shapes=[
            pltpu.VMEM((2, n - 1, parts, grain, K), F32),
            pltpu.VMEM((2, n - 1, parts, grain, K), F32),
            pltpu.VMEM((2, parts, grain, K), F32),
            pltpu.VMEM((tiles, tile, K), F32),
            pltpu.VMEM((nc, share, K), F32),
            pltpu.VMEM((nc, tiles, tile), F32),
            pltpu.VMEM((nc, K + 8, K), F32),
            pltpu.VMEM((nc, share, K), F32),
            dma((2, n - 1, parts)), dma((2, n - 1, parts)),
            dma((tiles,)), dma((nc, share // tile)),
            dma((nc - 1,)), dma((nc,)), dma((nc - 1,)), dma((nc,)),
            dma((nc - 1,)), dma((nc,)),
        ],
        compiler_params=pltpu.CompilerParams(collective_id=1, has_side_effects=True),
    )(src, mask, x.reshape(-1, grain, K), gb, residual, vb, jacobian)


def update_kernel(j_ref, u_ref, vt_ref, beta_ref, jr_ref, trial_ref, out_ref, corrected_ref):
    hi, lo = split(u_ref[...])
    twice = jnp.concatenate([hi, hi], axis=1)
    main = jnp.dot(twice, vt_ref[...], preferred_element_type=F32)
    rest = jnp.dot(lo, vt_ref[:K, :], preferred_element_type=F32)
    out_ref[...] = j_ref[...] + (main + rest)
    low_rank = jnp.sum(jnp.transpose(u_ref[...] * beta_ref[:1]), axis=0, keepdims=True)
    corrected_ref[...] = trial_ref[...] - (jr_ref[...] + low_rank)


def update(jacobian, u_rows, vt, beta, j_r, trial):
    rows, cols = jacobian.shape
    row = pl.BlockSpec((1, TILE), lambda i: (0, i))
    return pl.pallas_call(
        update_kernel,
        grid=(rows // TILE,),
        out_shape=(
            jax.ShapeDtypeStruct((rows, cols), F32),
            jax.ShapeDtypeStruct((1, rows), F32),
        ),
        in_specs=[
            pl.BlockSpec((TILE, cols), lambda i: (i, 0)),
            pl.BlockSpec((TILE, K), lambda i: (i, 0)),
            pl.BlockSpec((2 * K, cols), lambda i: (0, 0)),
            pl.BlockSpec((8, K), lambda i: (0, 0)),
            row,
            row,
        ],
        out_specs=(pl.BlockSpec((TILE, cols), lambda i: (i, 0)), row),
    )(jacobian, u_rows, vt, beta, j_r, trial)


def per_device(jacobian, diff_inputs, diff_outputs, face_dof, counts, residual, trial):
    row_block, col_block = jacobian.shape
    n_row, n_col = lax.axis_size("row"), lax.axis_size("col")
    col_at = lax.axis_index("col")
    runs = face_dof.shape[0] // UNIT
    first = jnp.arange(runs, dtype=jnp.int32) * UNIT
    run_unit = jnp.where(first < counts[0], face_dof.reshape(runs, UNIT)[:, 0] // UNIT, -1)

    part = min(UNIT, col_block // (2 * n_row))
    per_unit = UNIT // part
    granule = jnp.arange(col_block // part, dtype=jnp.int32)
    v_src, v_mask = lookup(run_unit, col_at * (col_block // UNIT) + granule // per_unit)
    v_src = v_src * per_unit + granule % per_unit

    share = row_block // n_col
    grain = min(UNIT, share // 2)
    per_share = share // grain
    piece = jnp.arange(n_row * per_share, dtype=jnp.int32)
    w_row = (piece // per_share) * row_block + col_at * share + (piece % per_share) * grain
    w_src, w_mask = lookup(run_unit, w_row // UNIT)
    w_src = w_src * (UNIT // grain) + (w_row % UNIT) // grain

    r_row = residual.reshape(1, col_block)
    vb, vt, gb = ring_sum(v_src, v_mask, diff_inputs, r_row, col_block, n_row)
    u, beta, j_r = products(
        jacobian, vb, gb, r_row, w_src, w_mask, diff_outputs, grain, n_row, n_col
    )
    updated, corrected = update(
        jacobian, u.reshape(row_block, K), vt, beta,
        j_r.reshape(1, row_block), trial.reshape(1, row_block),
    )
    return (updated, corrected[0])


def solution(mesh):
    placed = (
        P("row", "col"),
        P("row", None),
        P("row", None),
        P("row"),
        P("row"),
        P("col"),
        P("row"),
    )
    return jax.shard_map(
        per_device,
        mesh=mesh,
        in_specs=placed,
        out_specs=(P("row", "col"), P("row")),
        check_vma=False,
    )
```

profile of v0, /device:TPU:0, one launch (start us, length us, event | category | flops | bytes accessed | tf_op | source)
XLA Modules:
  0.0 141.6 jit_solution(5422645181254049116)
XLA Ops:
  1.3 0.8 slice_reduce_fusion
  2.1 0.2 compare_reduce_fusion
  2.3 0.7 fusion.1
  3.0 0.5 fusion.6.src_ref
  3.6 0.5 convert_element_type.7.mask_ref
  4.1 0.6 convert_element_type.6.mask_ref
  4.7 61.7 %shard_map.86 = (bf16[4096,256]{1,0:T(8,128)(2,1)}, bf16[256,4096]{1,0:T(8,128)(2,1)}, f32[136,128]{1,0:T(8,128)}) custom-call(s32[32]{0:T(128)} %get-tuple-element.20.src_ref, f32[32]{0:T(128)} %convert_element_type.7.mask_ref, f32[32,128,128]{2,1,0:T(8,128)} %bitcast.12, f32[1,4096]{1,0:T(1,128)} %bitcast.15), custom_call_target="tpu_custom_call" | custom-call | tf_op jit(solution)/shard_map/pallas_call | solution.py:126
  66.4 47.0 %shard_map.87 = (f32[4,512,128]{2,1,0:T(8,128)}, f32[8,128]{1,0:T(8,128)}, f32[8,256]{1,0:T(8,128)}) custom-call(s32[32]{0:T(128)} %fusion.6.src_ref, f32[32]{0:T(128)} %convert_element_type.6.mask_ref, f32[32,128,128]{2,1,0:T(8,128)} %bitcast.13, f32[136,128]{1,0:T(8,128)} %get-tuple-element.10.gb_ref, f32[1,4096]{1,0:T(1,128)} %bitcast.16, ...), custom_call_target="tpu_custom_call" | custom-call | tf_op jit(solution)/shard_map/pallas_call | solution.py:343
  113.4 1.3 copy.9
  114.7 26.9 %shard_map.88 = (f32[2048,4096]{1,0:T(8,128)}, f32[1,2048]{1,0:T(1,128)}) custom-call(f32[2048,4096]{1,0:T(8,128)} %j_ref.3, f32[2048,128]{1,0:T(8,128)} %bitcast.14, bf16[256,4096]{1,0:T(8,128)(2,1)} %get-tuple-element.13.vt_ref, f32[8,128]{1,0:T(8,128)} %get-tuple-element.14.beta_ref, f32[1,2048]{1,0:T(1,128)} %bitcast.17, f32[1,2048]{1,0:T(1,128)} %bitcast.19), custom_call_target="tpu_custom_call" | custom-call | tf_op jit(solution)/shard_map/pallas_call | solution.py:383
  (2 shorter events, 0.0 us)
where the time goes:
time: 142 us
  Pallas kernels  136 us (96%)
  other arithmetic  2.55 us (2%)
  local copies, waits for them, and re-layouts  2.12 us (1%)
    pallas_call x1, Pallas kernels, ring_sum(): pl.pallas_call(functools.partial(ring_kernel, n, parts), out_shape=(jax.S...  61.7 us
    pallas_call x1, Pallas kernels, products(): pl.pallas_call(functools.partial(product_kernel, n, nc, parts), grid=(til...  47 us
    pallas_call x1, Pallas kernels, update(): pl.pallas_call(update_kernel, grid=(rows // TILE,), out_shape=(jax.ShapeD...  26.9 us

commit v1 on v0

v1 whole, which is shorter than its diff:
```python
import functools

import jax
import jax.numpy as jnp
from jax import lax
from jax.experimental import pallas as pl
from jax.experimental.pallas import tpu as pltpu
from jax.sharding import PartitionSpec as P

K = 128
NS = 4
UNIT = 128
TILE = 256
VMEM_LIMIT = 26 * 2**20

HIGH = lax.Precision.HIGHEST
REG = 0.1
F32 = jnp.float32
BF16 = jnp.bfloat16
MESH = pl.DeviceIdType.MESH
VMEM_SPEC = pl.BlockSpec(memory_space=pltpu.VMEM)
ANY_SPEC = pl.BlockSpec(memory_space=pl.ANY)
SMEM_SPEC = pl.BlockSpec(memory_space=pltpu.SMEM)


def split(x):
    hi = x.astype(BF16)
    return hi, (x - hi.astype(F32)).astype(BF16)


def ring_place(index, n):
    return index // 2 + (index % 2) * (n - 1 - 2 * (index // 2))


def ring_index(place, n):
    side = place // (n // 2)
    level = place + side * (n - 1 - 2 * place)
    return 2 * level + side


def lookup(run_unit, wanted):
    hit = run_unit[None, :] == wanted[:, None]
    src = jnp.sum(jnp.where(hit, jnp.arange(run_unit.shape[0], dtype=jnp.int32)[None, :], 0), axis=1)
    return src.astype(jnp.int32), jnp.any(hit, axis=1).astype(F32)


def gather_kernel(
    n, nc, parts, w_parts, v_src, v_mask, w_src, w_mask, v_hbm, w_hbm, j_hbm, r_ref,
    j_ref, vt_ref, u_ref, beta_ref, jr_ref,
    xv, xw, whole, landed, sent, vb, gram, beta, jv,
    w_land, w_sent, jv_land, jv_sum, jr_all, gb, gb_all,
    load_sem, j_sem, v_send, v_recv, w_send, w_recv,
    jv_send, jv_recv, gb_send, gb_recv, jr_send, jr_recv, u_send, u_recv,
):
    rows, cols = j_ref.shape
    part = whole.shape[1]
    chunk = part * parts
    grain = w_land.shape[3]
    share = jv_land.shape[1]
    strips, j_rows = jr_ref.shape
    me = lax.axis_index("col")
    place = ring_place(lax.axis_index("row"), n)
    right = ring_index((place + 1) % n, n)
    left = ring_index((place + n - 1) % n, n)
    peers = [(me + k) % nc for k in range(1, nc)]

    def load(k):
        return pltpu.make_async_copy((v_hbm, w_hbm)[k], (xv, xw)[k], load_sem.at[k])

    def j_load(at):
        block = pl.ds(pl.multiple_of(at * j_rows, j_rows), j_rows)
        return pltpu.make_async_copy(j_hbm.at[block], j_ref.at[block], j_sem.at[at])

    load(0).start()
    load(1).start()
    for at in range(strips):
        j_load(at).start()

    barrier = pltpu.get_barrier_semaphore()
    for peer in (left, right):
        pl.semaphore_signal(barrier, inc=1, device_id={"row": peer}, device_id_type=MESH)
    for peer in peers:
        pl.semaphore_signal(barrier, inc=1, device_id={"col": peer}, device_id_type=MESH)
    gram[...] = jnp.zeros_like(gram)
    beta[...] = jnp.zeros_like(beta)
    jv[...] = jnp.zeros_like(jv)
    load(0).wait()
    pl.semaphore_wait(barrier, 2 + len(peers))

    def to_row(source, target, send, recv, way):
        return pltpu.make_async_remote_copy(
            src_ref=source, dst_ref=target, send_sem=send, recv_sem=recv,
            device_id={"row": right if way == 0 else left}, device_id_type=MESH,
        )

    def to_col(source, target, send, recv, peer):
        return pltpu.make_async_remote_copy(
            src_ref=source, dst_ref=target, send_sem=send, recv_sem=recv,
            device_id={"col": peer}, device_id_type=MESH,
        )

    order = [(p, way) for p in range(parts) for way in range(2)]

    def granule(way, back, p):
        sign = 1 if way == 0 else -1
        at = (place + 2 * n - sign * back) % n
        return (way * n + at) * parts + p

    def own(at):
        return xv[v_src[at]] * v_mask[at]

    def reduce_copy(step, way, p):
        return to_row(
            sent.at[way, step, p], landed.at[way, step, p],
            v_send.at[way, step, p], v_recv.at[way, step, p], way,
        )

    def spread_copy(step, way, p, at):
        return to_row(
            whole.at[at], whole.at[at], v_send.at[way, step, p], v_recv.at[way, step, p], way
        )

    def w_copy(step, way, p):
        return to_row(
            w_sent.at[way, step, p], w_land.at[way, step, p],
            w_send.at[way, step, p], w_recv.at[way, step, p], way,
        )

    def w_own(step, way, p):
        sign = 1 if way == 0 else -1
        block = ring_index((place + 2 * n - sign * (step + 1)) % n, n)
        at = (block * 2 + way) * w_parts + p
        return xw[w_src[at]] * w_mask[at]

    def times_residual(at):
        j_load(at).wait()
        strip = min(64, j_rows)
        sums = []
        for sub in range(j_rows // strip):
            block = pl.ds(pl.multiple_of(at * j_rows + sub * strip, strip), strip)
            total = jnp.zeros((strip, K), F32)
            for c in range(0, cols, K):
                total = total + j_ref[block, c : c + K] * r_ref[:, c : c + K]
            sums.append(total)
        total = jnp.concatenate(sums, axis=0)
        jr_all[me, pl.ds(at, 1), :] = jnp.sum(jnp.transpose(total), axis=0, keepdims=True)

    def absorb(block, off, width):
        at = pl.ds(pl.multiple_of(off, width), width)
        hi, lo = split(block)
        both = jnp.concatenate([hi, lo], axis=1)
        vb[at, :] = both
        t_hi, t_lo = split(jnp.transpose(block))
        vt_ref[:K, at] = t_hi
        vt_ref[K:, at] = t_lo
        gram[...] += lax.dot_general(
            both, both, (((0,), (0,)), ((), ())), preferred_element_type=F32
        )
        r_hi, r_lo = split(jnp.broadcast_to(r_ref[:, at], (8, width)))
        beta[...] += jnp.dot(
            jnp.concatenate([r_hi, r_lo], axis=0), both, preferred_element_type=F32
        )

    def accumulate(off, width, first, count):
        tile = min(TILE, count)
        at = pl.ds(pl.multiple_of(off, width), width)

        def body(t, carry):
            block = pl.ds(pl.multiple_of(first + t * tile, tile), tile)
            hi, lo = split(j_ref[block, at])
            both = jnp.dot(
                jnp.concatenate([hi, lo], axis=0), vb[at, :], preferred_element_type=F32
            )
            jv[block, :] += both[:tile, :K] + (both[:tile, K:] + both[tile:, :K]) + both[tile:, K:]
            return carry

        lax.fori_loop(0, count // tile, body, 0)

    piped = chunk % UNIT == 0

    def work(step, p, way):
        if not piped:
            return
        off = granule(way, step, 0) * part
        if p == 0:
            first = pl.multiple_of(granule(way, step, 0), parts)
            absorb(whole[pl.ds(first, parts)].reshape(chunk, K), off, chunk)
        accumulate(off, chunk, p * (rows // parts), rows // parts)

    for p, way in order:
        sent[way, 0, p] = own(granule(way, 0, p))
        reduce_copy(0, way, p).start()
    times_residual(0)

    def reduce_step(step, carry):
        for p, way in order:
            reduce_copy(step - 1, way, p).wait_recv()
            sent[way, step, p] = own(granule(way, step, p)) + landed[way, step - 1, p]
            reduce_copy(step, way, p).start()
        if strips < n - 1:
            pl.when(step < strips)(lambda: times_residual(step))
        else:
            times_residual(step)
        return carry

    lax.fori_loop(1, n - 1, reduce_step, 0)

    for p, way in order:
        reduce_copy(n - 2, way, p).wait_recv()
        at = granule(way, n - 1, p)
        whole[at] = own(at) + landed[way, n - 2, p]
        spread_copy(n - 1, way, p, at).start()
    for at in range(n - 1, strips):
        times_residual(at)

    def jr_copy(k, slot):
        return to_col(jr_all.at[slot], jr_all.at[slot], jr_send.at[k], jr_recv.at[slot], peers[k])

    for k in range(nc - 1):
        jr_copy(k, me).start()

    def spread_step(step, carry):
        for p, way in order:
            at = granule(way, step, p)
            spread_copy(step - 1, way, p, at).wait_recv()
            spread_copy(step, way, p, at).start()
            work(step - 1, p, way)
        return carry

    last = 2 * (n - 1)
    lax.fori_loop(n, last, spread_step, 0)

    w_order = [(p, way) for p in range(w_parts) for way in range(2)]
    load(1).wait()
    for p, way in w_order:
        w_sent[way, 0, p] = w_own(0, way, p)
        w_copy(0, way, p).start()

    for p, way in order:
        spread_copy(last - 1, way, p, granule(way, last, p)).wait_recv()
        work(last - 1, p, way)
    for p, way in order:
        work(last, p, way)
    if not piped:
        per_unit = UNIT // part
        for unit in range(cols // UNIT):
            block = jnp.concatenate([whole[unit * per_unit + s] for s in range(per_unit)], axis=0)
            absorb(block, unit * UNIT, UNIT)
        for off in range(0, cols, 2 * UNIT):
            accumulate(off, 2 * UNIT, 0, rows)

    gb[:K, :] = gram[:K, :K] + (gram[:K, K:] + gram[K:, :K]) + gram[K:, K:]
    gb[K:, :] = beta[:8, :K] + (beta[:8, K:] + beta[8:, :K])

    def gb_copy(k, slot):
        return to_col(gb, gb_all.at[slot], gb_send.at[k], gb_recv.at[slot], peers[k])

    def jv_copy(k, slot, owner):
        block = pl.ds(pl.multiple_of(owner * share, share), share)
        return to_col(jv.at[block], jv_land.at[slot], jv_send.at[k], jv_recv.at[slot], peers[k])

    for k in range(nc - 1):
        gb_copy(k, me).start()
    for k in range(nc - 1):
        jv_copy(k, me, peers[k]).start()

    def w_step(step):
        for p, way in w_order:
            w_copy(step - 1, way, p).wait_recv()
            w_sent[way, step, p] = w_own(step, way, p) + w_land[way, step - 1, p]
            w_copy(step, way, p).start()

    def regularise():
        for k in range(nc - 1):
            gb_copy(k, peers[k]).wait_recv()
        gb_all[me] = gb[...]
        sums = gb_all[0]
        for slot in range(1, nc):
            sums = sums + gb_all[slot]
        beta_ref[...] = sums[K:]
        total = sums[:K]
        trace = jnp.sum(jnp.sum(total * eye, axis=0, keepdims=True), axis=1, keepdims=True)
        regular = total + REG * (trace / K) * eye
        norm_one = jnp.max(
            jnp.sum(jnp.abs(regular), axis=0, keepdims=True), axis=1, keepdims=True
        )
        return regular, regular / (norm_one * norm_one)

    eye = (
        lax.broadcasted_iota(jnp.int32, (K, K), 0) == lax.broadcasted_iota(jnp.int32, (K, K), 1)
    ).astype(F32)
    begin = min(2, n - 2)
    for step in range(1, n - 1):
        w_step(step)
        if step == begin:
            regular, zmat = regularise()
            sweeps = 0
        if step >= begin:
            until = NS if step == n - 2 else min(NS, step - begin + 1)
            for sweep in range(sweeps, until):
                inner = jnp.dot(regular, zmat, precision=HIGH, preferred_element_type=F32)
                zmat = jnp.dot(
                    zmat, 2.0 * eye - inner, precision=HIGH, preferred_element_type=F32
                )
            sweeps = until

    for k in range(nc - 1):
        jv_copy(k, peers[k], me).wait_recv()
    jv_land[me] = jv[pl.ds(pl.multiple_of(me * share, share), share), :]
    total = jv_land[0]
    for slot in range(1, nc):
        total = total + jv_land[slot]
    jv_sum[...] = total

    for k in range(nc - 1):
        jr_copy(k, peers[k]).wait_recv()
    jr_sum = jr_all[0]
    for slot in range(1, nc):
        jr_sum = jr_sum + jr_all[slot]
    jr_ref[...] = jr_sum

    partner = me + 1 - 2 * (me % 2)
    half = nc // 2

    def u_copy(slot, hop, at, peer):
        block = u_ref.at[slot, pl.ds(at * grain, grain)]
        return to_col(block, block, u_send.at[hop, at], u_recv.at[slot, at], peer)

    for p, way in w_order:
        at = way * w_parts + p
        block = pl.ds(at * grain, grain)
        w_copy(n - 2, way, p).wait_recv()
        value = w_own(n - 1, way, p) + w_land[way, n - 2, p]
        u_ref[me, block] = jnp.dot(
            value - jv_sum[block, :], zmat, precision=HIGH, preferred_element_type=F32
        )
        for k in range(1, half):
            u_copy(me, k - 1, at, (me + 2 * k) % nc).start()
        u_copy(me, half - 1, at, partner).start()
    for p, way in w_order:
        at = way * w_parts + p
        for k in range(1, half):
            slot = (me + 2 * k) % nc
            u_copy(slot, half - 1 + k, at, partner).wait_recv()
            u_copy(slot, half - 1 + k, at, partner).start()
    for p, way in w_order:
        at = way * w_parts + p
        for k in range(half):
            u_copy((partner + 2 * k) % nc, 0, at, partner).wait_recv()

    for p, way in w_order:
        for hop in range(nc - 1):
            u_copy(me, hop, way * w_parts + p, partner).wait_send()
    for k in range(nc - 1):
        gb_copy(k, me).wait_send()
        jr_copy(k, me).wait_send()
        jv_copy(k, me, peers[k]).wait_send()

    def drain(step, carry):
        for p, way in order:
            reduce_copy(step, way, p).wait_send()
            spread_copy(step + n - 1, way, p, granule(way, 0, p)).wait_send()
        for p, way in w_order:
            w_copy(step, way, p).wait_send()
        return carry

    lax.fori_loop(0, n - 1, drain, 0)


def gather(v_src, v_mask, w_src, w_mask, diff_inputs, diff_outputs, jacobian, residual, n, nc):
    rows, cols = jacobian.shape
    chunk = cols // (2 * n)
    part = min(UNIT, chunk)
    parts = chunk // part
    share = rows // nc
    grain = min(UNIT, share // 2)
    w_parts = share // (2 * grain)
    strips = min(n, rows // UNIT)
    runs = diff_inputs.shape[0]
    dma = pltpu.SemaphoreType.DMA
    v = pltpu.VMEM
    return pl.pallas_call(
        functools.partial(gather_kernel, n, nc, parts, w_parts),
        out_shape=(
            v((rows, cols), F32),
            v((2 * K, cols), BF16),
            v((nc, share, K), F32),
            v((8, K), F32),
            v((strips, rows // strips), F32),
        ),
        in_specs=[SMEM_SPEC] * 4 + [ANY_SPEC] * 3 + [VMEM_SPEC],
        out_specs=(VMEM_SPEC,) * 5,
        scratch_shapes=[
            v((runs // part, part, K), F32),
            v((runs // grain, grain, K), F32),
            v((cols // part, part, K), F32),
            v((2, n - 1, parts, part, K), F32),
            v((2, n - 1, parts, part, K), F32),
            v((cols, 2 * K), BF16),
            v((2 * K, 2 * K), F32),
            v((16, 2 * K), F32),
            v((rows, K), F32),
            v((2, n - 1, w_parts, grain, K), F32),
            v((2, n - 1, w_parts, grain, K), F32),
            v((nc, share, K), F32),
            v((share, K), F32),
            v((nc, strips, rows // strips), F32),
            v((K + 8, K), F32),
            v((nc, K + 8, K), F32),
            dma((2,)), dma((strips,)),
            dma((2, 2 * (n - 1), parts)), dma((2, 2 * (n - 1), parts)),
            dma((2, n - 1, w_parts)), dma((2, n - 1, w_parts)),
            dma((nc - 1,)), dma((nc,)), dma((nc - 1,)), dma((nc,)),
            dma((nc - 1,)), dma((nc,)),
            dma((nc - 1, share // grain)), dma((nc, share // grain)),
        ],
        compiler_params=pltpu.CompilerParams(
            collective_id=0, has_side_effects=True, vmem_limit_bytes=VMEM_LIMIT
        ),
    )(
        v_src, v_mask, w_src, w_mask,
        diff_inputs.reshape(-1, part, K), diff_outputs.reshape(-1, grain, K), jacobian, residual,
    )


def update_kernel(j_ref, vt_ref, u_ref, beta_ref, jr_ref, trial_ref, out_ref, corrected_ref):
    at = pl.program_id(0)
    tile = out_ref.shape[0]
    block = pl.ds(pl.multiple_of(at * tile, tile), tile)
    u = u_ref[block, :]
    hi, lo = split(u)
    twice = jnp.concatenate([hi, hi], axis=1)
    main = jnp.dot(twice, vt_ref[...], preferred_element_type=F32)
    rest = jnp.dot(lo, vt_ref[:K, :], preferred_element_type=F32)
    out_ref[...] = j_ref[block, :] + (main + rest)
    low_rank = jnp.sum(jnp.transpose(u * beta_ref[:1]), axis=0, keepdims=True)
    corrected_ref[...] = trial_ref[...] - (jr_ref[pl.ds(at, 1), :] + low_rank)


def update(jacobian, vt, u, beta, j_r, trial):
    rows, cols = jacobian.shape
    tile = j_r.shape[1]
    row = pl.BlockSpec((1, tile), lambda i: (0, i))
    held = [pltpu.with_memory_space_constraint(x, pltpu.VMEM) for x in (jacobian, vt, u, beta, j_r)]
    return pl.pallas_call(
        update_kernel,
        grid=(rows // tile,),
        out_shape=(
            jax.ShapeDtypeStruct((rows, cols), F32),
            jax.ShapeDtypeStruct((1, rows), F32),
        ),
        in_specs=[VMEM_SPEC] * 5 + [row],
        out_specs=(pl.BlockSpec((tile, cols), lambda i: (i, 0)), row),
        compiler_params=pltpu.CompilerParams(vmem_limit_bytes=VMEM_LIMIT),
    )(*held, trial)


def per_device(jacobian, diff_inputs, diff_outputs, face_dof, counts, residual, trial):
    row_block, col_block = jacobian.shape
    n_row, n_col = lax.axis_size("row"), lax.axis_size("col")
    col_at = lax.axis_index("col")
    runs = face_dof.shape[0] // UNIT
    first = jnp.arange(runs, dtype=jnp.int32) * UNIT
    run_unit = jnp.where(first < counts[0], face_dof.reshape(runs, UNIT)[:, 0] // UNIT, -1)

    part = min(UNIT, col_block // (2 * n_row))
    per_unit = UNIT // part
    granule = jnp.arange(col_block // part, dtype=jnp.int32)
    v_src, v_mask = lookup(run_unit, col_at * (col_block // UNIT) + granule // per_unit)
    v_src = v_src * per_unit + granule % per_unit

    share = row_block // n_col
    grain = min(UNIT, share // 2)
    per_share = share // grain
    piece = jnp.arange(n_row * per_share, dtype=jnp.int32)
    w_row = (piece // per_share) * row_block + col_at * share + (piece % per_share) * grain
    w_src, w_mask = lookup(run_unit, w_row // UNIT)
    w_src = w_src * (UNIT // grain) + (w_row % UNIT) // grain

    held, vt, u, beta, j_r = gather(
        v_src, v_mask, w_src, w_mask, diff_inputs, diff_outputs, jacobian,
        residual.reshape(1, col_block), n_row, n_col,
    )
    updated, corrected = update(
        held, vt, u.reshape(row_block, K), beta, j_r, trial.reshape(1, row_block)
    )
    return (updated, corrected[0])


def solution(mesh):
    placed = (
        P("row", "col"),
        P("row", None),
        P("row", None),
        P("row"),
        P("row"),
        P("col"),
        P("row"),
    )
    return jax.shard_map(
        per_device,
        mesh=mesh,
        in_specs=placed,
        out_specs=(P("row", "col"), P("row")),
        check_vma=False,
    )
```

time: 142 us -> 128 us (0.901)
  Pallas kernels: 136 us -> 123 us
    pallas_call x3 -> x2, Pallas kernels: 136 us -> 123 us  [the longest x1 108 us: gather(): pl.pallas_call(functools.partial(gather_kernel, n, nc, parts, w_parts), o...]
where the time goes in v1:
time: 128 us
  Pallas kernels  123 us (96%)
  other arithmetic  2.53 us (2%)
  between operations  1.31 us (1%)
    pallas_call x1, Pallas kernels, gather(): pl.pallas_call(functools.partial(gather_kernel, n, nc, parts, w_parts), o...  108 us
    pallas_call x1, Pallas kernels, update(): pl.pallas_call(update_kernel, grid=(rows // tile,), out_shape=(jax.ShapeD...  15.1 us

profile of v1, /device:TPU:0, one launch (start us, length us, event | category | flops | bytes accessed | tf_op | source)
XLA Modules:
  0.0 127.9 jit_solution(6285971876959044029)
XLA Ops:
  1.3 0.8 slice_reduce_fusion
  2.1 0.2 compare_reduce_fusion
  2.3 0.7 fusion.1
  3.0 0.6 fusion.6.w_src
  3.6 0.5 convert_element_type.7.w_mask
  4.1 0.5 convert_element_type.6.v_mask
  4.7 108.1 %shard_map.86 = (f32[2048,4096]{1,0:T(8,128)S(1)}, bf16[256,4096]{1,0:T(8,128)(2,1)S(1)}, f32[4,512,128]{2,1,0:T(8,128)S(1)}, f32[8,128]{1,0:T(8,128)S(1)}, f32[8,256]{1,0:T(8,128)S(1)}) custom-call(s32[32]{0:T(128)} %get-tuple-element.19.v_src, f32[32]{0:T(128)} %convert_element_type.6.v_mask, s32[32]{0:T(128)} %fusion.6.w_src, ...), custom_call_target="tpu_custom_call" | custom-call | tf_op jit(solution)/shard_map/pallas_call | solution.py:382
  112.8 15.1 %shard_map.87 = (f32[2048,4096]{1,0:T(8,128)}, f32[1,2048]{1,0:T(1,128)}) custom-call(f32[2048,4096]{1,0:T(8,128)S(1)} %get-tuple-element.9.j_ref, bf16[256,4096]{1,0:T(8,128)(2,1)S(1)} %get-tuple-element.10.vt_ref, f32[2048,128]{1,0:T(8,128)S(1)} %bitcast.9, f32[8,128]{1,0:T(8,128)S(1)} %get-tuple-element.12.beta_ref, ...), custom_call_target="tpu_custom_call" | custom-call | tf_op jit(solution)/shard_map/pallas_call | solution.py:445
  (2 shorter events, 0.0 us)

commit v2 on v1

--- a/solution.py
+++ b/solution.py
@@ -10,7 +10,9 @@
 K = 128
 NS = 4
 UNIT = 128
-TILE = 256
+PART = 64
+TILE = 1024
+WIDTH = 256
 VMEM_LIMIT = 26 * 2**20
 
 HIGH = lax.Precision.HIGHEST
@@ -38,16 +40,10 @@
     return 2 * level + side
 
 
-def lookup(run_unit, wanted):
-    hit = run_unit[None, :] == wanted[:, None]
-    src = jnp.sum(jnp.where(hit, jnp.arange(run_unit.shape[0], dtype=jnp.int32)[None, :], 0), axis=1)
-    return src.astype(jnp.int32), jnp.any(hit, axis=1).astype(F32)
-
-
 def gather_kernel(
-    n, nc, parts, w_parts, v_src, v_mask, w_src, w_mask, v_hbm, w_hbm, j_hbm, r_ref,
+    n, nc, parts, w_parts, dof_ref, count_ref, v_hbm, w_hbm, j_hbm, r_ref,
     j_ref, vt_ref, u_ref, beta_ref, jr_ref,
-    xv, xw, whole, landed, sent, vb, gram, beta, jv,
+    run_unit, xv, xw, whole, landed, sent, vb, gram, beta, jv,
     w_land, w_sent, jv_land, jv_sum, jr_all, gb, gb_all,
     load_sem, j_sem, v_send, v_recv, w_send, w_recv,
     jv_send, jv_recv, gb_send, gb_recv, jr_send, jr_recv, u_send, u_recv,
@@ -67,23 +63,25 @@
     def load(k):
         return pltpu.make_async_copy((v_hbm, w_hbm)[k], (xv, xw)[k], load_sem.at[k])
 
-    def j_load(at):
-        block = pl.ds(pl.multiple_of(at * j_rows, j_rows), j_rows)
+    pieces = 2 * parts
+
+    def j_load(at, piece=0, count=1):
+        size = j_rows // count
+        block = pl.ds(pl.multiple_of(at * j_rows + piece * size, size), size)
         return pltpu.make_async_copy(j_hbm.at[block], j_ref.at[block], j_sem.at[at])
 
     load(0).start()
-    load(1).start()
-    for at in range(strips):
-        j_load(at).start()
+    j_load(0).start()
 
     barrier = pltpu.get_barrier_semaphore()
     for peer in (left, right):
         pl.semaphore_signal(barrier, inc=1, device_id={"row": peer}, device_id_type=MESH)
     for peer in peers:
         pl.semaphore_signal(barrier, inc=1, device_id={"col": peer}, device_id_type=MESH)
-    gram[...] = jnp.zeros_like(gram)
-    beta[...] = jnp.zeros_like(beta)
-    jv[...] = jnp.zeros_like(jv)
+    runs = run_unit.shape[0]
+    for at in range(runs):
+        unit = lax.shift_right_logical(dof_ref[at * UNIT], UNIT.bit_length() - 1)
+        run_unit[at] = jnp.where(at * UNIT < count_ref[0], unit, -1)
     load(0).wait()
     pl.semaphore_wait(barrier, 2 + len(peers))
 
@@ -106,8 +104,32 @@
         at = (place + 2 * n - sign * back) % n
         return (way * n + at) * parts + p
 
-    def own(at):
-        return xv[v_src[at]] * v_mask[at]
+    def locate(unit):
+        src = jnp.int32(-1)
+        for at in range(runs):
+            src = jnp.where(run_unit[at] == unit, at, src)
+        return jnp.maximum(src, 0), (src >= 0).astype(F32)
+
+    def pick(source, rows_at):
+        size = source.shape[1]
+        per_unit = UNIT // size
+        found, values = {}, []
+        for at, same in rows_at:
+            if same is None or same not in found:
+                found[same] = locate(at // per_unit)
+            src, mask = found[same]
+            values.append(lambda src=src, mask=mask, at=at: source[src * per_unit + at % per_unit] * mask)
+        return values
+
+    def sharing(p, way, count, size):
+        per_unit = UNIT // size
+        return (way, p // per_unit) if count % per_unit == 0 else None
+
+    def own(step):
+        base = me * (cols // part)
+        return pick(
+            xv, [(base + granule(way, step, p), sharing(p, way, parts, part)) for p, way in order]
+        )
 
     def reduce_copy(step, way, p):
         return to_row(
@@ -126,11 +148,16 @@
             w_send.at[way, step, p], w_recv.at[way, step, p], way,
         )
 
-    def w_own(step, way, p):
-        sign = 1 if way == 0 else -1
-        block = ring_index((place + 2 * n - sign * (step + 1)) % n, n)
-        at = (block * 2 + way) * w_parts + p
-        return xw[w_src[at]] * w_mask[at]
+    w_order = [(p, way) for p in range(w_parts) for way in range(2)]
+
+    def w_own(step):
+        wanted = []
+        for p, way in w_order:
+            sign = 1 if way == 0 else -1
+            block = ring_index((place + 2 * n - sign * (step + 1)) % n, n)
+            at = (block * rows + me * share) // grain + way * w_parts + p
+            wanted.append((at, sharing(p, way, w_parts, grain)))
+        return pick(xw, wanted)
 
     def times_residual(at):
         j_load(at).wait()
@@ -161,56 +188,70 @@
             jnp.concatenate([r_hi, r_lo], axis=0), both, preferred_element_type=F32
         )
 
-    def accumulate(off, width, first, count):
+    def accumulate(offs, width, first, count):
         tile = min(TILE, count)
-        at = pl.ds(pl.multiple_of(off, width), width)
-
-        def body(t, carry):
-            block = pl.ds(pl.multiple_of(first + t * tile, tile), tile)
-            hi, lo = split(j_ref[block, at])
+        ats = [pl.ds(pl.multiple_of(off, width), width) for off in offs]
+        for t in range(count // tile):
+            block = pl.ds(first + t * tile, tile)
+            hi, lo = split(jnp.concatenate([j_ref[block, at] for at in ats], axis=1))
             both = jnp.dot(
-                jnp.concatenate([hi, lo], axis=0), vb[at, :], preferred_element_type=F32
+                jnp.concatenate([hi, lo], axis=0),
+                jnp.concatenate([vb[at, :] for at in ats], axis=0),
+                preferred_element_type=F32,
             )
             jv[block, :] += both[:tile, :K] + (both[:tile, K:] + both[tile:, :K]) + both[tile:, K:]
-            return carry
-
-        lax.fori_loop(0, count // tile, body, 0)
 
     piped = chunk % UNIT == 0
 
     def work(step, p, way):
         if not piped:
             return
-        off = granule(way, step, 0) * part
+        offs = [granule(w, step, 0) * part for w in range(2)]
         if p == 0:
             first = pl.multiple_of(granule(way, step, 0), parts)
-            absorb(whole[pl.ds(first, parts)].reshape(chunk, K), off, chunk)
-        accumulate(off, chunk, p * (rows // parts), rows // parts)
-
-    for p, way in order:
-        sent[way, 0, p] = own(granule(way, 0, p))
+            absorb(whole[pl.ds(first, parts)].reshape(chunk, K), offs[way], chunk)
+        half_at = {(parts // 2 - 1, 1): 0, (parts - 1, 1): 1}.get((p, way))
+        if half_at is not None:
+            accumulate(offs, chunk, half_at * (rows // 2), rows // 2)
+
+    for (p, way), value in zip(order, own(0)):
+        sent[way, 0, p] = value()
         reduce_copy(0, way, p).start()
-    times_residual(0)
+    gram[...] = jnp.zeros_like(gram)
+    beta[...] = jnp.zeros_like(beta)
+    jv[...] = jnp.zeros_like(jv)
 
     def reduce_step(step, carry):
-        for p, way in order:
+        def load_piece(at):
+            j_load(step, at, pieces).start()
+
+        values = own(step)
+        for at, (p, way) in enumerate(order):
             reduce_copy(step - 1, way, p).wait_recv()
-            sent[way, step, p] = own(granule(way, step, p)) + landed[way, step - 1, p]
+            sent[way, step, p] = values[at]() + landed[way, step - 1, p]
             reduce_copy(step, way, p).start()
-        if strips < n - 1:
-            pl.when(step < strips)(lambda: times_residual(step))
+            if strips < n - 1:
+                pl.when(step < strips)(functools.partial(load_piece, at))
+            else:
+                load_piece(at)
+        if strips < n - 2:
+            pl.when(step <= strips)(lambda: times_residual(step - 1))
         else:
-            times_residual(step)
+            times_residual(step - 1)
         return carry
 
     lax.fori_loop(1, n - 1, reduce_step, 0)
 
-    for p, way in order:
+    values = own(n - 1)
+    for at, (p, way) in enumerate(order):
         reduce_copy(n - 2, way, p).wait_recv()
-        at = granule(way, n - 1, p)
-        whole[at] = own(at) + landed[way, n - 2, p]
-        spread_copy(n - 1, way, p, at).start()
-    for at in range(n - 1, strips):
+        spot = granule(way, n - 1, p)
+        whole[spot] = values[at]() + landed[way, n - 2, p]
+        spread_copy(n - 1, way, p, spot).start()
+        if strips == n:
+            j_load(n - 1, at, pieces).start()
+    load(1).start()
+    for at in range(n - 2, strips):
         times_residual(at)
 
     def jr_copy(k, slot):
@@ -230,10 +271,9 @@
     last = 2 * (n - 1)
     lax.fori_loop(n, last, spread_step, 0)
 
-    w_order = [(p, way) for p in range(w_parts) for way in range(2)]
     load(1).wait()
-    for p, way in w_order:
-        w_sent[way, 0, p] = w_own(0, way, p)
+    for (p, way), value in zip(w_order, w_own(0)):
+        w_sent[way, 0, p] = value()
         w_copy(0, way, p).start()
 
     for p, way in order:
@@ -247,7 +287,7 @@
             block = jnp.concatenate([whole[unit * per_unit + s] for s in range(per_unit)], axis=0)
             absorb(block, unit * UNIT, UNIT)
         for off in range(0, cols, 2 * UNIT):
-            accumulate(off, 2 * UNIT, 0, rows)
+            accumulate([off, off + UNIT], UNIT, 0, rows)
 
     gb[:K, :] = gram[:K, :K] + (gram[:K, K:] + gram[K:, :K]) + gram[K:, K:]
     gb[K:, :] = beta[:8, :K] + (beta[:8, K:] + beta[8:, :K])
@@ -265,9 +305,9 @@
         jv_copy(k, me, peers[k]).start()
 
     def w_step(step):
-        for p, way in w_order:
+        for (p, way), value in zip(w_order, w_own(step)):
             w_copy(step - 1, way, p).wait_recv()
-            w_sent[way, step, p] = w_own(step, way, p) + w_land[way, step - 1, p]
+            w_sent[way, step, p] = value() + w_land[way, step - 1, p]
             w_copy(step, way, p).start()
 
     def regularise():
@@ -326,17 +366,28 @@
         block = u_ref.at[slot, pl.ds(at * grain, grain)]
         return to_col(block, block, u_send.at[hop, at], u_recv.at[slot, at], peer)
 
-    for p, way in w_order:
-        at = way * w_parts + p
-        block = pl.ds(at * grain, grain)
-        w_copy(n - 2, way, p).wait_recv()
-        value = w_own(n - 1, way, p) + w_land[way, n - 2, p]
-        u_ref[me, block] = jnp.dot(
-            value - jv_sum[block, :], zmat, precision=HIGH, preferred_element_type=F32
-        )
-        for k in range(1, half):
-            u_copy(me, k - 1, at, (me + 2 * k) % nc).start()
-        u_copy(me, half - 1, at, partner).start()
+    z_hi, z_lo = split(zmat)
+    z_both = jnp.concatenate([z_hi, z_lo], axis=1)
+    values = w_own(n - 1)
+    for p in range(w_parts):
+        ats = [way * w_parts + p for way in range(2)]
+        diffs = []
+        for way in range(2):
+            w_copy(n - 2, way, p).wait_recv()
+            block = pl.ds(ats[way] * grain, grain)
+            diffs.append(values[2 * p + way]() + w_land[way, n - 2, p] - jv_sum[block, :])
+        d_hi, d_lo = split(jnp.concatenate(diffs, axis=0))
+        both = jnp.dot(
+            jnp.concatenate([d_hi, d_lo], axis=0), z_both, preferred_element_type=F32
+        )
+        size = 2 * grain
+        u = both[:size, :K] + (both[:size, K:] + both[size:, :K]) + both[size:, K:]
+        for way in range(2):
+            at = ats[way]
+            u_ref[me, pl.ds(at * grain, grain)] = u[way * grain : (way + 1) * grain]
+            for k in range(1, half):
+                u_copy(me, k - 1, at, (me + 2 * k) % nc).start()
+            u_copy(me, half - 1, at, partner).start()
     for p, way in w_order:
         at = way * w_parts + p
         for k in range(1, half):
@@ -367,13 +418,13 @@
     lax.fori_loop(0, n - 1, drain, 0)
 
 
-def gather(v_src, v_mask, w_src, w_mask, diff_inputs, diff_outputs, jacobian, residual, n, nc):
+def gather(face_dof, counts, diff_inputs, diff_outputs, jacobian, residual, n, nc):
     rows, cols = jacobian.shape
     chunk = cols // (2 * n)
-    part = min(UNIT, chunk)
+    part = min(PART, chunk)
     parts = chunk // part
     share = rows // nc
-    grain = min(UNIT, share // 2)
+    grain = min(PART, share // 2)
     w_parts = share // (2 * grain)
     strips = min(n, rows // UNIT)
     runs = diff_inputs.shape[0]
@@ -388,9 +439,10 @@
             v((8, K), F32),
             v((strips, rows // strips), F32),
         ),
-        in_specs=[SMEM_SPEC] * 4 + [ANY_SPEC] * 3 + [VMEM_SPEC],
+        in_specs=[SMEM_SPEC] * 2 + [ANY_SPEC] * 3 + [VMEM_SPEC],
         out_specs=(VMEM_SPEC,) * 5,
         scratch_shapes=[
+            pltpu.SMEM((runs // UNIT,), jnp.int32),
             v((runs // part, part, K), F32),
             v((runs // grain, grain, K), F32),
             v((cols // part, part, K), F32),
@@ -418,68 +470,74 @@
             collective_id=0, has_side_effects=True, vmem_limit_bytes=VMEM_LIMIT
         ),
     )(
-        v_src, v_mask, w_src, w_mask,
+        face_dof, counts,
         diff_inputs.reshape(-1, part, K), diff_outputs.reshape(-1, grain, K), jacobian, residual,
     )
 
 
-def update_kernel(j_ref, vt_ref, u_ref, beta_ref, jr_ref, trial_ref, out_ref, corrected_ref):
-    at = pl.program_id(0)
-    tile = out_ref.shape[0]
-    block = pl.ds(pl.multiple_of(at * tile, tile), tile)
-    u = u_ref[block, :]
-    hi, lo = split(u)
-    twice = jnp.concatenate([hi, hi], axis=1)
-    main = jnp.dot(twice, vt_ref[...], preferred_element_type=F32)
-    rest = jnp.dot(lo, vt_ref[:K, :], preferred_element_type=F32)
-    out_ref[...] = j_ref[block, :] + (main + rest)
-    low_rank = jnp.sum(jnp.transpose(u * beta_ref[:1]), axis=0, keepdims=True)
-    corrected_ref[...] = trial_ref[...] - (jr_ref[pl.ds(at, 1), :] + low_rank)
+def update_kernel(
+    j_ref, vt_ref, u_ref, beta_ref, jr_ref, trial_ref, out_ref, corrected_ref,
+    twice, low, stage, sem,
+):
+    rows, cols = j_ref.shape
+    slots, _, width = stage.shape
+    hi, lo = split(u_ref[...])
+    twice[:, :K] = hi
+    twice[:, K:] = hi
+    low[...] = lo
+
+    def copy(at):
+        columns = pl.ds(pl.multiple_of(at * width, width), width)
+        slot = at % slots
+        return pltpu.make_async_copy(stage.at[slot], out_ref.at[:, columns], sem.at[slot])
+
+    def step(at, carry):
+        pl.when(at >= slots)(lambda: copy(at - slots).wait())
+        columns = pl.ds(pl.multiple_of(at * width, width), width)
+        main = jnp.dot(twice[...], vt_ref[:, columns], preferred_element_type=F32)
+        rest = jnp.dot(low[...], vt_ref[:K, columns], preferred_element_type=F32)
+        stage[at % slots] = j_ref[:, columns] + (main + rest)
+        copy(at).start()
+        return carry
+
+    count = cols // width
+    lax.fori_loop(0, count, step, 0)
+    low_rank = jnp.sum(jnp.transpose(u_ref[...] * beta_ref[:1]), axis=0, keepdims=True)
+    size = jr_ref.shape[1]
+    for at in range(jr_ref.shape[0]):
+        block = slice(at * size, (at + 1) * size)
+        corrected_ref[:, block] = trial_ref[:, block] - (jr_ref[at : at + 1, :] + low_rank[:, block])
+    for at in range(count - slots, count):
+        copy(at).wait()
 
 
 def update(jacobian, vt, u, beta, j_r, trial):
     rows, cols = jacobian.shape
-    tile = j_r.shape[1]
-    row = pl.BlockSpec((1, tile), lambda i: (0, i))
     held = [pltpu.with_memory_space_constraint(x, pltpu.VMEM) for x in (jacobian, vt, u, beta, j_r)]
+    slots = 3
     return pl.pallas_call(
         update_kernel,
-        grid=(rows // tile,),
         out_shape=(
             jax.ShapeDtypeStruct((rows, cols), F32),
             jax.ShapeDtypeStruct((1, rows), F32),
         ),
-        in_specs=[VMEM_SPEC] * 5 + [row],
-        out_specs=(pl.BlockSpec((tile, cols), lambda i: (i, 0)), row),
+        in_specs=[VMEM_SPEC] * 6,
+        out_specs=(ANY_SPEC, VMEM_SPEC),
+        scratch_shapes=[
+            pltpu.VMEM((rows, 2 * K), BF16),
+            pltpu.VMEM((rows, K), BF16),
+            pltpu.VMEM((slots, rows, WIDTH), F32),
+            pltpu.SemaphoreType.DMA((slots,)),
+        ],
         compiler_params=pltpu.CompilerParams(vmem_limit_bytes=VMEM_LIMIT),
     )(*held, trial)
 
 
 def per_device(jacobian, diff_inputs, diff_outputs, face_dof, counts, residual, trial):
     row_block, col_block = jacobian.shape
-    n_row, n_col = lax.axis_size("row"), lax.axis_size("col")
-    col_at = lax.axis_index("col")
-    runs = face_dof.shape[0] // UNIT
-    first = jnp.arange(runs, dtype=jnp.int32) * UNIT
-    run_unit = jnp.where(first < counts[0], face_dof.reshape(runs, UNIT)[:, 0] // UNIT, -1)
-
-    part = min(UNIT, col_block // (2 * n_row))
-    per_unit = UNIT // part
-    granule = jnp.arange(col_block // part, dtype=jnp.int32)
-    v_src, v_mask = lookup(run_unit, col_at * (col_block // UNIT) + granule // per_unit)
-    v_src = v_src * per_unit + granule % per_unit
-
-    share = row_block // n_col
-    grain = min(UNIT, share // 2)
-    per_share = share // grain
-    piece = jnp.arange(n_row * per_share, dtype=jnp.int32)
-    w_row = (piece // per_share) * row_block + col_at * share + (piece % per_share) * grain
-    w_src, w_mask = lookup(run_unit, w_row // UNIT)
-    w_src = w_src * (UNIT // grain) + (w_row % UNIT) // grain
-
     held, vt, u, beta, j_r = gather(
-        v_src, v_mask, w_src, w_mask, diff_inputs, diff_outputs, jacobian,
-        residual.reshape(1, col_block), n_row, n_col,
+        face_dof, counts, diff_inputs, diff_outputs, jacobian,
+        residual.reshape(1, col_block), lax.axis_size("row"), lax.axis_size("col"),
     )
     updated, corrected = update(
         held, vt, u.reshape(row_block, K), beta, j_r, trial.reshape(1, row_block)

time: 128 us -> 102 us (0.80)
  Pallas kernels: 123 us -> 101 us
  other arithmetic: 2.53 us -> 0 us
    pallas_call x1, Pallas kernels: 108 us -> 86.2 us  [gather(): pl.pallas_call(functools.partial(gather_kernel, n, nc, parts, w_parts), o...]
where the time goes in v2:
time: 102 us
  Pallas kernels  101 us (99%)
  between operations  1.29 us (1%)
    pallas_call x1, Pallas kernels, gather(): pl.pallas_call(functools.partial(gather_kernel, n, nc, parts, w_parts), o...  86.2 us
    pallas_call x1, Pallas kernels, update(): pl.pallas_call(update_kernel, out_shape=(jax.ShapeDtypeStruct((rows, cols...  14.3 us

profile of v2, /device:TPU:0, one launch (start us, length us, event | category | flops | bytes accessed | tf_op | source)
XLA Modules:
  0.0 101.9 jit_solution(12502123148492639390)
XLA Ops:
  1.3 86.2 %shard_map.86 = (f32[2048,4096]{1,0:T(8,128)S(1)}, bf16[256,4096]{1,0:T(8,128)(2,1)S(1)}, f32[4,512,128]{2,1,0:T(8,128)S(1)}, f32[8,128]{1,0:T(8,128)S(1)}, f32[8,256]{1,0:T(8,128)S(1)}) custom-call(s32[4096]{0:T(1024)} %dof_ref.1, s32[1]{0:T(128)S(6)} %copy.9.count_ref, f32[64,64,128]{2,1,0:T(8,128)} %bitcast.7, f32[64,64,128]{2,1,0:T(8,128)} %bitcast.8, ...), custom_call_target="tpu_custom_call" | custom-call | tf_op jit(solution)/shard_map/pallas_call | solution.py:433
  87.5 14.3 %shard_map.87 = (f32[2048,4096]{1,0:T(8,128)}, f32[1,2048]{1,0:T(1,128)}) custom-call(f32[2048,4096]{1,0:T(8,128)S(1)} %get-tuple-element.9.j_ref, bf16[256,4096]{1,0:T(8,128)(2,1)S(1)} %get-tuple-element.10.vt_ref, f32[2048,128]{1,0:T(8,128)S(1)} %bitcast.6, f32[8,128]{1,0:T(8,128)S(1)} %get-tuple-element.12.beta_ref, ...), custom_call_target="tpu_custom_call" | custom-call | tf_op jit(solution)/shard_map/pallas_call | solution.py:518

commit v3 on v2

--- a/solution.py
+++ b/solution.py
@@ -12,7 +12,7 @@
 UNIT = 128
 PART = 64
 TILE = 1024
-WIDTH = 256
+WIDTH = 512
 VMEM_LIMIT = 26 * 2**20
 
 HIGH = lax.Precision.HIGHEST
@@ -22,7 +22,6 @@
 MESH = pl.DeviceIdType.MESH
 VMEM_SPEC = pl.BlockSpec(memory_space=pltpu.VMEM)
 ANY_SPEC = pl.BlockSpec(memory_space=pl.ANY)
-SMEM_SPEC = pl.BlockSpec(memory_space=pltpu.SMEM)
 
 
 def split(x):
@@ -41,9 +40,9 @@
 
 
 def gather_kernel(
-    n, nc, parts, w_parts, dof_ref, count_ref, v_hbm, w_hbm, j_hbm, r_ref,
+    n, nc, parts, w_parts, dof_hbm, count_hbm, v_hbm, w_hbm, j_hbm, r_hbm,
     j_ref, vt_ref, u_ref, beta_ref, jr_ref,
-    run_unit, xv, xw, whole, landed, sent, vb, gram, beta, jv,
+    dof_ref, count_ref, run_unit, r_ref, xv, xw, whole, landed, sent, vb, gram, beta, jv,
     w_land, w_sent, jv_land, jv_sum, jr_all, gb, gb_all,
     load_sem, j_sem, v_send, v_recv, w_send, w_recv,
     jv_send, jv_recv, gb_send, gb_recv, jr_send, jr_recv, u_send, u_recv,
@@ -61,7 +60,10 @@
     peers = [(me + k) % nc for k in range(1, nc)]
 
     def load(k):
-        return pltpu.make_async_copy((v_hbm, w_hbm)[k], (xv, xw)[k], load_sem.at[k])
+        source = (v_hbm, w_hbm, dof_hbm, count_hbm, r_hbm)[k]
+        return pltpu.make_async_copy(
+            source, (xv, xw, dof_ref, count_ref, r_ref)[k], load_sem.at[k]
+        )
 
     pieces = 2 * parts
 
@@ -70,8 +72,8 @@
         block = pl.ds(pl.multiple_of(at * j_rows + piece * size, size), size)
         return pltpu.make_async_copy(j_hbm.at[block], j_ref.at[block], j_sem.at[at])
 
-    load(0).start()
-    j_load(0).start()
+    for k in (2, 3, 0, 4):
+        load(k).start()
 
     barrier = pltpu.get_barrier_semaphore()
     for peer in (left, right):
@@ -79,10 +81,14 @@
     for peer in peers:
         pl.semaphore_signal(barrier, inc=1, device_id={"col": peer}, device_id_type=MESH)
     runs = run_unit.shape[0]
+    load(2).wait()
+    load(3).wait()
     for at in range(runs):
         unit = lax.shift_right_logical(dof_ref[at * UNIT], UNIT.bit_length() - 1)
         run_unit[at] = jnp.where(at * UNIT < count_ref[0], unit, -1)
     load(0).wait()
+    load(4).wait()
+    j_load(0).start()
     pl.semaphore_wait(barrier, 2 + len(peers))
 
     def to_row(source, target, send, recv, way):
@@ -150,9 +156,9 @@
 
     w_order = [(p, way) for p in range(w_parts) for way in range(2)]
 
-    def w_own(step):
+    def w_own(step, some):
         wanted = []
-        for p, way in w_order:
+        for p, way in some:
             sign = 1 if way == 0 else -1
             block = ring_index((place + 2 * n - sign * (step + 1)) % n, n)
             at = (block * rows + me * share) // grain + way * w_parts + p
@@ -265,20 +271,36 @@
             at = granule(way, step, p)
             spread_copy(step - 1, way, p, at).wait_recv()
             spread_copy(step, way, p, at).start()
+            reduce_copy(step - n, way, p).wait_send()
             work(step - 1, p, way)
         return carry
 
     last = 2 * (n - 1)
-    lax.fori_loop(n, last, spread_step, 0)
+    lax.fori_loop(n, last - 1, spread_step, 0)
+
+    def w_step(step):
+        for (p, way), value in zip(w_order, w_own(step, w_order)):
+            if step == 0:
+                w_sent[way, 0, p] = value()
+            else:
+                w_copy(step - 1, way, p).wait_recv()
+                w_sent[way, step, p] = value() + w_land[way, step - 1, p]
+            w_copy(step, way, p).start()
+        for p, way in order:
+            if step > 0:
+                spread_copy(n + step - 2, way, p, granule(way, 0, p)).wait_send()
+        for p, way in w_order:
+            if step > 1:
+                w_copy(step - 2, way, p).wait_send()
 
     load(1).wait()
-    for (p, way), value in zip(w_order, w_own(0)):
-        w_sent[way, 0, p] = value()
-        w_copy(0, way, p).start()
-
+    w_step(0)
+    spread_step(last - 1, 0)
+    w_step(1)
     for p, way in order:
         spread_copy(last - 1, way, p, granule(way, last, p)).wait_recv()
         work(last - 1, p, way)
+    w_step(2)
     for p, way in order:
         work(last, p, way)
     if not piped:
@@ -303,12 +325,6 @@
         gb_copy(k, me).start()
     for k in range(nc - 1):
         jv_copy(k, me, peers[k]).start()
-
-    def w_step(step):
-        for (p, way), value in zip(w_order, w_own(step)):
-            w_copy(step - 1, way, p).wait_recv()
-            w_sent[way, step, p] = value() + w_land[way, step - 1, p]
-            w_copy(step, way, p).start()
 
     def regularise():
         for k in range(nc - 1):
@@ -329,20 +345,16 @@
     eye = (
         lax.broadcasted_iota(jnp.int32, (K, K), 0) == lax.broadcasted_iota(jnp.int32, (K, K), 1)
     ).astype(F32)
-    begin = min(2, n - 2)
-    for step in range(1, n - 1):
-        w_step(step)
-        if step == begin:
+    sweeps = 0
+    for step in range(2, n - 2):
+        w_step(step + 1)
+        if step == 2:
             regular, zmat = regularise()
-            sweeps = 0
-        if step >= begin:
-            until = NS if step == n - 2 else min(NS, step - begin + 1)
-            for sweep in range(sweeps, until):
-                inner = jnp.dot(regular, zmat, precision=HIGH, preferred_element_type=F32)
-                zmat = jnp.dot(
-                    zmat, 2.0 * eye - inner, precision=HIGH, preferred_element_type=F32
-                )
-            sweeps = until
+        until = NS if step == n - 3 else min(NS, step - 1)
+        for sweep in range(sweeps, until):
+            inner = jnp.dot(regular, zmat, precision=HIGH, preferred_element_type=F32)
+            zmat = jnp.dot(zmat, 2.0 * eye - inner, precision=HIGH, preferred_element_type=F32)
+        sweeps = until
 
     for k in range(nc - 1):
         jv_copy(k, peers[k], me).wait_recv()
@@ -368,26 +380,40 @@
 
     z_hi, z_lo = split(zmat)
     z_both = jnp.concatenate([z_hi, z_lo], axis=1)
-    values = w_own(n - 1)
-    for p in range(w_parts):
-        ats = [way * w_parts + p for way in range(2)]
-        diffs = []
-        for way in range(2):
-            w_copy(n - 2, way, p).wait_recv()
-            block = pl.ds(ats[way] * grain, grain)
-            diffs.append(values[2 * p + way]() + w_land[way, n - 2, p] - jv_sum[block, :])
-        d_hi, d_lo = split(jnp.concatenate(diffs, axis=0))
-        both = jnp.dot(
-            jnp.concatenate([d_hi, d_lo], axis=0), z_both, preferred_element_type=F32
-        )
-        size = 2 * grain
-        u = both[:size, :K] + (both[:size, K:] + both[size:, :K]) + both[size:, K:]
-        for way in range(2):
-            at = ats[way]
-            u_ref[me, pl.ds(at * grain, grain)] = u[way * grain : (way + 1) * grain]
-            for k in range(1, half):
-                u_copy(me, k - 1, at, (me + 2 * k) % nc).start()
-            u_copy(me, half - 1, at, partner).start()
+
+    def finish(some):
+        values = dict(zip(some, w_own(n - 1, some)))
+        for p in sorted({p for p, way in some}):
+            ats = [way * w_parts + p for way in range(2)]
+            diffs = []
+            for way in range(2):
+                w_copy(n - 2, way, p).wait_recv()
+                block = pl.ds(ats[way] * grain, grain)
+                diffs.append(values[p, way]() + w_land[way, n - 2, p] - jv_sum[block, :])
+            d_hi, d_lo = split(jnp.concatenate(diffs, axis=0))
+            both = jnp.dot(
+                jnp.concatenate([d_hi, d_lo], axis=0), z_both, preferred_element_type=F32
+            )
+            size = 2 * grain
+            u = both[:size, :K] + (both[:size, K:] + both[size:, :K]) + both[size:, K:]
+            for way in range(2):
+                at = ats[way]
+                u_ref[me, pl.ds(at * grain, grain)] = u[way * grain : (way + 1) * grain]
+                for k in range(1, half):
+                    u_copy(me, k - 1, at, (me + 2 * k) % nc).start()
+                u_copy(me, half - 1, at, partner).start()
+
+    for p, way in order:
+        reduce_copy(n - 2, way, p).wait_send()
+        spread_copy(last - 1, way, p, granule(way, 0, p)).wait_send()
+    for p, way in w_order:
+        w_copy(n - 3, way, p).wait_send()
+    for k in range(nc - 1):
+        gb_copy(k, me).wait_send()
+        jr_copy(k, me).wait_send()
+        jv_copy(k, me, peers[k]).wait_send()
+
+    finish(w_order)
     for p, way in w_order:
         at = way * w_parts + p
         for k in range(1, half):
@@ -402,20 +428,8 @@
     for p, way in w_order:
         for hop in range(nc - 1):
             u_copy(me, hop, way * w_parts + p, partner).wait_send()
-    for k in range(nc - 1):
-        gb_copy(k, me).wait_send()
-        jr_copy(k, me).wait_send()
-        jv_copy(k, me, peers[k]).wait_send()
-
-    def drain(step, carry):
-        for p, way in order:
-            reduce_copy(step, way, p).wait_send()
-            spread_copy(step + n - 1, way, p, granule(way, 0, p)).wait_send()
-        for p, way in w_order:
-            w_copy(step, way, p).wait_send()
-        return carry
-
-    lax.fori_loop(0, n - 1, drain, 0)
+    for p, way in w_order:
+        w_copy(n - 2, way, p).wait_send()
 
 
 def gather(face_dof, counts, diff_inputs, diff_outputs, jacobian, residual, n, nc):
@@ -439,10 +453,13 @@
             v((8, K), F32),
             v((strips, rows // strips), F32),
         ),
-        in_specs=[SMEM_SPEC] * 2 + [ANY_SPEC] * 3 + [VMEM_SPEC],
+        in_specs=[ANY_SPEC] * 6,
         out_specs=(VMEM_SPEC,) * 5,
         scratch_shapes=[
+            pltpu.SMEM((runs,), jnp.int32),
+            pltpu.SMEM((1,), jnp.int32),
             pltpu.SMEM((runs // UNIT,), jnp.int32),
+            v((1, cols), F32),
             v((runs // part, part, K), F32),
             v((runs // grain, grain, K), F32),
             v((cols // part, part, K), F32),
@@ -459,7 +476,7 @@
             v((nc, strips, rows // strips), F32),
             v((K + 8, K), F32),
             v((nc, K + 8, K), F32),
-            dma((2,)), dma((strips,)),
+            dma((5,)), dma((strips,)),
             dma((2, 2 * (n - 1), parts)), dma((2, 2 * (n - 1), parts)),
             dma((2, n - 1, w_parts)), dma((2, n - 1, w_parts)),
             dma((nc - 1,)), dma((nc,)), dma((nc - 1,)), dma((nc,)),

time: 102 us -> 101 us (level)
  Pallas kernels: 101 us -> 98.9 us
    pallas_call x1, Pallas kernels: 86.2 us -> 85.1 us  [gather(): pl.pallas_call(functools.partial(gather_kernel, n, nc, parts, w_parts), o...]
where the time goes in v3:
time: 101 us; the launch traced here: 100 us
  Pallas kernels  98.9 us (98%)
  between operations  1.45 us (1%)
    pallas_call x1, Pallas kernels, gather(): pl.pallas_call(functools.partial(gather_kernel, n, nc, parts, w_parts), o...  85.1 us
    pallas_call x1, Pallas kernels, update(): pl.pallas_call(update_kernel, out_shape=(jax.ShapeDtypeStruct((rows, cols...  13.8 us

profile of v3, /device:TPU:0, one launch (start us, length us, event | category | flops | bytes accessed | tf_op | source)
XLA Modules:
  0.0 100.4 jit_solution(15291530080075220739)
XLA Ops:
  1.3 85.1 %shard_map.86 = (f32[2048,4096]{1,0:T(8,128)S(1)}, bf16[256,4096]{1,0:T(8,128)(2,1)S(1)}, f32[4,512,128]{2,1,0:T(8,128)S(1)}, f32[8,128]{1,0:T(8,128)S(1)}, f32[8,256]{1,0:T(8,128)S(1)}) custom-call(s32[4096]{0:T(1024)} %dof_hbm.1, s32[1]{0:T(128)S(6)} %copy.9.count_hbm, f32[64,64,128]{2,1,0:T(8,128)} %bitcast.7, f32[64,64,128]{2,1,0:T(8,128)} %bitcast.8, ...), custom_call_target="tpu_custom_call" | custom-call | tf_op jit(solution)/shard_map/pallas_call | solution.py:447
  86.4 13.8 %shard_map.87 = (f32[2048,4096]{1,0:T(8,128)}, f32[1,2048]{1,0:T(1,128)}) custom-call(f32[2048,4096]{1,0:T(8,128)S(1)} %get-tuple-element.9.j_ref, bf16[256,4096]{1,0:T(8,128)(2,1)S(1)} %get-tuple-element.10.vt_ref, f32[2048,128]{1,0:T(8,128)S(1)} %bitcast.6, f32[8,128]{1,0:T(8,128)S(1)} %get-tuple-element.12.beta_ref, ...), custom_call_target="tpu_custom_call" | custom-call | tf_op jit(solution)/shard_map/pallas_call | solution.py:535

commit v4 on v3

--- a/solution.py
+++ b/solution.py
@@ -43,7 +43,7 @@
     n, nc, parts, w_parts, dof_hbm, count_hbm, v_hbm, w_hbm, j_hbm, r_hbm,
     j_ref, vt_ref, u_ref, beta_ref, jr_ref,
     dof_ref, count_ref, run_unit, r_ref, xv, xw, whole, landed, sent, vb, gram, beta, jv,
-    w_land, w_sent, jv_land, jv_sum, jr_all, gb, gb_all,
+    w_land, w_sent, jv_land, jv_sum, jr_all, gb, gb_all, twice, low,
     load_sem, j_sem, v_send, v_recv, w_send, w_recv,
     jv_send, jv_recv, gb_send, gb_recv, jr_send, jr_recv, u_send, u_recv,
 ):
@@ -375,7 +375,7 @@
     half = nc // 2
 
     def u_copy(slot, hop, at, peer):
-        block = u_ref.at[slot, pl.ds(at * grain, grain)]
+        block = u_ref.at[slot, pl.ds(pl.multiple_of(at * grain, grain), grain)]
         return to_col(block, block, u_send.at[hop, at], u_recv.at[slot, at], peer)
 
     z_hi, z_lo = split(zmat)
@@ -414,15 +414,36 @@
         jv_copy(k, me, peers[k]).wait_send()
 
     finish(w_order)
-    for p, way in w_order:
-        at = way * w_parts + p
+    grains = 2 * w_parts
+    for at in range(grains):
+        u_copy(partner, 0, at, partner).wait_recv()
+    pair = me // 2
+    hi, lo = split(u_ref[pl.ds(2 * pair, 2)].reshape(2 * share, K))
+    twice[:, :K] = hi
+    twice[:, K:] = hi
+    low[...] = lo
+    near = pl.ds(pl.multiple_of(pair * 2 * share, 2 * share), 2 * share)
+    width = cols // grains
+
+    def pass_on(index, carry):
+        at = (index % 2) * w_parts + index // 2
         for k in range(1, half):
             slot = (me + 2 * k) % nc
             u_copy(slot, half - 1 + k, at, partner).wait_recv()
             u_copy(slot, half - 1 + k, at, partner).start()
-    for p, way in w_order:
-        at = way * w_parts + p
-        for k in range(half):
+
+        @pl.when(index < grains // 2)
+        def _():
+            columns = pl.ds(pl.multiple_of(index * width, width), width)
+            main = jnp.dot(twice[...], vt_ref[:, columns], preferred_element_type=F32)
+            rest = jnp.dot(low[...], vt_ref[:K, columns], preferred_element_type=F32)
+            j_ref[near, columns] += main + rest
+
+        return carry
+
+    lax.fori_loop(0, grains, pass_on, 0)
+    for at in range(grains):
+        for k in range(1, half):
             u_copy((partner + 2 * k) % nc, 0, at, partner).wait_recv()
 
     for p, way in w_order:
@@ -476,6 +497,8 @@
             v((nc, strips, rows // strips), F32),
             v((K + 8, K), F32),
             v((nc, K + 8, K), F32),
+            v((2 * share, 2 * K), BF16),
+            v((2 * share, K), BF16),
             dma((5,)), dma((strips,)),
             dma((2, 2 * (n - 1), parts)), dma((2, 2 * (n - 1), parts)),
             dma((2, n - 1, w_parts)), dma((2, n - 1, w_parts)),
@@ -493,58 +516,95 @@
 
 
 def update_kernel(
-    j_ref, vt_ref, u_ref, beta_ref, jr_ref, trial_ref, out_ref, corrected_ref,
-    twice, low, stage, sem,
+    nc, j_ref, vt_ref, u_ref, beta_ref, jr_ref, trial_hbm, out_ref, corrected_hbm,
+    trial, corrected, twice, low, stage, whole_sem, stage_sem, small_sem,
 ):
     rows, cols = j_ref.shape
-    slots, _, width = stage.shape
-    hi, lo = split(u_ref[...])
-    twice[:, :K] = hi
-    twice[:, K:] = hi
-    low[...] = lo
+    slots, size, width = stage.shape
+    pairs = nc // 2
+    pair = lax.axis_index("col") // 2
+    pieces = whole_sem.shape[0]
+    piece = size // pieces
+
+    def ready(at):
+        block = pl.ds(pl.multiple_of(pair * size + at * piece, piece), piece)
+        half = pl.ds(0, cols // 2)
+        return pltpu.make_async_copy(
+            j_ref.at[block, half], out_ref.at[block, half], whole_sem.at[at]
+        )
+
+    for at in range(pieces):
+        ready(at).start()
+    load = pltpu.make_async_copy(trial_hbm, trial, small_sem.at[0])
+    load.start()
+    per = cols // width
+    done = per // 2
+    count = per * pairs - done
+
+    def place(at):
+        at = at + done
+        other = (pair + at // per) % pairs
+        block = pl.ds(pl.multiple_of(other * size, size), size)
+        return block, pl.ds(pl.multiple_of((at % per) * width, width), width)
 
     def copy(at):
-        columns = pl.ds(pl.multiple_of(at * width, width), width)
-        slot = at % slots
-        return pltpu.make_async_copy(stage.at[slot], out_ref.at[:, columns], sem.at[slot])
+        return pltpu.make_async_copy(
+            stage.at[at % slots], out_ref.at[place(at)], stage_sem.at[at % slots]
+        )
 
     def step(at, carry):
         pl.when(at >= slots)(lambda: copy(at - slots).wait())
-        columns = pl.ds(pl.multiple_of(at * width, width), width)
+        block, columns = place(at)
+
+        @pl.when((at == 0) | ((at + done) % per == 0))
+        def _():
+            hi, lo = split(u_ref[block, :])
+            twice[:, :K] = hi
+            twice[:, K:] = hi
+            low[...] = lo
+
         main = jnp.dot(twice[...], vt_ref[:, columns], preferred_element_type=F32)
         rest = jnp.dot(low[...], vt_ref[:K, columns], preferred_element_type=F32)
-        stage[at % slots] = j_ref[:, columns] + (main + rest)
+        stage[at % slots] = j_ref[block, columns] + (main + rest)
         copy(at).start()
         return carry
 
-    count = cols // width
     lax.fori_loop(0, count, step, 0)
     low_rank = jnp.sum(jnp.transpose(u_ref[...] * beta_ref[:1]), axis=0, keepdims=True)
-    size = jr_ref.shape[1]
+    load.wait()
+    strip = jr_ref.shape[1]
     for at in range(jr_ref.shape[0]):
-        block = slice(at * size, (at + 1) * size)
-        corrected_ref[:, block] = trial_ref[:, block] - (jr_ref[at : at + 1, :] + low_rank[:, block])
-    for at in range(count - slots, count):
+        block = slice(at * strip, (at + 1) * strip)
+        corrected[:, block] = trial[:, block] - (jr_ref[at : at + 1, :] + low_rank[:, block])
+    store = pltpu.make_async_copy(corrected, corrected_hbm, small_sem.at[1])
+    store.start()
+    for at in range(pieces):
+        ready(at).wait()
+    for at in range(max(0, count - slots), count):
         copy(at).wait()
-
-
-def update(jacobian, vt, u, beta, j_r, trial):
+    store.wait()
+
+
+def update(jacobian, vt, u, beta, j_r, trial, nc):
     rows, cols = jacobian.shape
     held = [pltpu.with_memory_space_constraint(x, pltpu.VMEM) for x in (jacobian, vt, u, beta, j_r)]
-    slots = 3
+    slots, size, pieces = 4, 2 * rows // nc, 4
+    dma = pltpu.SemaphoreType.DMA
     return pl.pallas_call(
-        update_kernel,
+        functools.partial(update_kernel, nc),
         out_shape=(
             jax.ShapeDtypeStruct((rows, cols), F32),
             jax.ShapeDtypeStruct((1, rows), F32),
         ),
-        in_specs=[VMEM_SPEC] * 6,
-        out_specs=(ANY_SPEC, VMEM_SPEC),
+        in_specs=[VMEM_SPEC] * 5 + [ANY_SPEC],
+        out_specs=(ANY_SPEC, ANY_SPEC),
         scratch_shapes=[
-            pltpu.VMEM((rows, 2 * K), BF16),
-            pltpu.VMEM((rows, K), BF16),
-            pltpu.VMEM((slots, rows, WIDTH), F32),
-            pltpu.SemaphoreType.DMA((slots,)),
+            pltpu.VMEM((1, rows), F32),
+            pltpu.VMEM((1, rows), F32),
+            pltpu.VMEM((size, 2 * K), BF16),
+            pltpu.VMEM((size, K), BF16),
+            pltpu.VMEM((slots, size, WIDTH), F32),
+            dma((pieces,)), dma((slots,)), dma((2,)),
         ],
         compiler_params=pltpu.CompilerParams(vmem_limit_bytes=VMEM_LIMIT),
     )(*held, trial)
@@ -557,7 +617,8 @@
         residual.reshape(1, col_block), lax.axis_size("row"), lax.axis_size("col"),
     )
     updated, corrected = update(
-        held, vt, u.reshape(row_block, K), beta, j_r, trial.reshape(1, row_block)
+        held, vt, u.reshape(row_block, K), beta, j_r, trial.reshape(1, row_block),
+        lax.axis_size("col"),
     )
     return (updated, corrected[0])
 

time: 101 us -> 98 us (0.970)
  Pallas kernels: 98.9 us -> 96.3 us
    pallas_call x1, Pallas kernels: 13.8 us -> 11.2 us  [update(): pl.pallas_call(functools.partial(update_kernel, nc), out_shape=(jax.Shape...]
where the time goes in v4:
time: 98 us; the launch traced here: 97.8 us
  Pallas kernels  96.3 us (98%)
  between operations  1.45 us (1%)
    pallas_call x1, Pallas kernels, gather(): pl.pallas_call(functools.partial(gather_kernel, n, nc, parts, w_parts), o...  85.1 us
    pallas_call x1, Pallas kernels, update(): pl.pallas_call(functools.partial(update_kernel, nc), out_shape=(jax.Shape...  11.2 us

profile of v4, /device:TPU:0, one launch (start us, length us, event | category | flops | bytes accessed | tf_op | source)
XLA Modules:
  0.0 97.8 jit_solution(11318943840560988882)
XLA Ops:
  1.3 85.1 %shard_map.86 = (f32[2048,4096]{1,0:T(8,128)S(1)}, bf16[256,4096]{1,0:T(8,128)(2,1)S(1)}, f32[4,512,128]{2,1,0:T(8,128)S(1)}, f32[8,128]{1,0:T(8,128)S(1)}, f32[8,256]{1,0:T(8,128)S(1)}) custom-call(s32[4096]{0:T(1024)} %dof_hbm.1, s32[1]{0:T(128)S(6)} %copy.9.count_hbm, f32[64,64,128]{2,1,0:T(8,128)} %bitcast.7, f32[64,64,128]{2,1,0:T(8,128)} %bitcast.8, ...), custom_call_target="tpu_custom_call" | custom-call | tf_op jit(solution)/shard_map/pallas_call | solution.py:468
  86.4 11.2 %shard_map.87 = (f32[2048,4096]{1,0:T(8,128)}, f32[1,2048]{1,0:T(1,128)}) custom-call(f32[2048,4096]{1,0:T(8,128)S(1)} %get-tuple-element.9.j_ref, bf16[256,4096]{1,0:T(8,128)(2,1)S(1)} %get-tuple-element.10.vt_ref, f32[2048,128]{1,0:T(8,128)S(1)} %bitcast.6, f32[8,128]{1,0:T(8,128)S(1)} %get-tuple-element.12.beta_ref, ...), custom_call_target="tpu_custom_call" | custom-call | tf_op jit(solution)/shard_map/pallas_call | solution.py:593
